TPU v7x, 32 devices: a whole 2x2x4 slice. The times are simulated.
32 devices in a mesh: group: 4 (over x, core), tensor: 4 (over z), dp: 2 (over y).
Axes of the slice: x: 2, y: 2, z: 4, core: 2. Of those that a mesh axis runs over, the one named last changes fastest.
Arguments:
- doc_emb: bfloat16 [48, 4096], P('group', 'dp'), may hold values from -6 to 6
- row_emb: bfloat16 [64, 4096], P(None, 'dp'), may hold values from -6 to 6
- hyper_in: bfloat16 [4096, 8192], P('dp', 'tensor'), may hold values from -0.09375 to 0.09375
- hyper_out: bfloat16 [8192, 8192], P('tensor', 'dp'), may hold values from -0.0625 to 0.0625
- assign: int32 [48], replicated, may hold values from 0 to 47, each once
- states: bfloat16 [2304, 8192], P('group', 'tensor'), may hold values from -6 to 6
- proj_weight: bfloat16 [8192, 8192], P('tensor', 'dp'), may hold values from -0.0625 to 0.0625
- targets: bfloat16 [2304, 8192], P(('group', 'tensor'), 'dp'), may hold values from -6 to 6
Outputs:
- adapted: bfloat16 [2304, 8192], P(('group', 'tensor'), 'dp')
- grad_down: float32 [48, 32, 8192], P('group', None, 'tensor')
- grad_up: float32 [48, 32, 8192], P('group', None, ('dp', 'tensor'))
Inputs may be any that keep to these rules, and one draw needn't show every extreme that they name: `assign`: every document is named by exactly one slot.
All inputs are finite; a program needn't handle non-finite values.
Results may differ from a plain program's by a relative error of at most 0.02.
Values may be sent and summed in bfloat16 or wider, within the bound.
No kernel may reach another device: no remote copies, remote signals or barrier semaphores. Data moves between devices by JAX's collectives and lax.ppermute only.
A program may use at most 128 MiB of HBM per device.

v0:
```python
import math
import jax
import jax.numpy as jnp
from jax import lax
from jax.sharding import PartitionSpec as P

D = 8192
R = 32
LOWDIM_MULTIPLE = 0.1


def spread(block, axis, owner):
    block = jnp.where(lax.axis_index(axis) == owner, block, jnp.zeros_like(block))
    return lax.psum(block, axis)


def hypernet(doc_rows, row_emb, hyper_in, hyper_out):
    doc_count = doc_rows.shape[0]
    pre_doc, pre_row = (
        lax.psum(
            jnp.dot(doc_rows, hyper_in, preferred_element_type=jnp.float32).astype(jnp.bfloat16),
            "dp",
        ).astype(jnp.float32),
        lax.psum(
            jnp.dot(row_emb, hyper_in, preferred_element_type=jnp.float32).astype(jnp.bfloat16),
            "dp",
        ).astype(jnp.float32),
    )
    hidden = jax.nn.silu(pre_doc[:, None, :] + pre_row[None, :, :]).astype(jnp.bfloat16)
    hidden = hidden.reshape(doc_count * 2 * R, hidden.shape[2])
    partial_value = jnp.dot(hidden, hyper_out, preferred_element_type=jnp.float32)
    summed = lax.psum(partial_value.astype(jnp.bfloat16), "tensor")
    factors = summed.reshape(doc_count, 2 * R, hyper_out.shape[1])
    ratio_axes = lax.axis_size("tensor") // lax.axis_size("dp")
    owner_rows = spread(factors[:, :R, :], "dp", lax.axis_index("tensor") // ratio_axes)
    col_width = hyper_out.shape[1] // ratio_axes
    down_block = lax.dynamic_slice_in_dim(
        owner_rows, lax.axis_index("tensor") % ratio_axes * col_width, col_width, 2
    )
    return (down_block, factors[:, R:, :])


def body(doc_emb, row_emb, hyper_in, hyper_out, assign, states, proj_weight, targets):
    doc_count = doc_emb.shape[0]
    group_start = lax.axis_index("group") * doc_count
    slot_docs = lax.dynamic_slice_in_dim(assign, group_start, doc_count)
    everyone = lax.all_gather(doc_emb, "group", axis=0, tiled=True)
    picker = (slot_docs[:, None] == jnp.arange(everyone.shape[0], dtype=jnp.int32)[None, :]).astype(
        jnp.bfloat16
    )
    chosen = jnp.dot(picker, everyone, preferred_element_type=jnp.float32).astype(jnp.bfloat16)
    slot_down, slot_up_factor = hypernet(chosen, row_emb, hyper_in, hyper_out)
    token_count = states.shape[0]
    per_doc = token_count // doc_count
    fan_width_multiplier = 1.0 / math.sqrt(D)
    bundled_entries = states.reshape(doc_count, per_doc, states.shape[1])
    low_part = jnp.einsum(
        "quw,qlw->qul", bundled_entries, slot_down, preferred_element_type=jnp.float32
    ).reshape(token_count, R)
    base_part = jnp.dot(states, proj_weight, preferred_element_type=jnp.float32)
    frozen_output, low_sum = (
        lax.psum_scatter(
            base_part.astype(jnp.bfloat16), "tensor", scatter_dimension=0, tiled=True
        ).astype(jnp.float32),
        lax.psum_scatter(
            low_part.astype(jnp.bfloat16), "tensor", scatter_dimension=0, tiled=True
        ).astype(jnp.float32),
    )
    row_count = frozen_output.shape[0]
    row_start = lax.axis_index("tensor") * row_count
    owner_doc = (row_start + jnp.arange(row_count, dtype=jnp.int32)) // per_doc
    document_member = owner_doc[:, None] == jnp.arange(doc_count, dtype=jnp.int32)[None, :]
    narrow_basis_map = (low_sum * fan_width_multiplier).astype(jnp.bfloat16)
    broadcast_rows = jnp.where(
        document_member[:, :, None], narrow_basis_map[:, None, :], jnp.zeros((), jnp.bfloat16)
    ).reshape(row_count, doc_count * R)
    up_factor_rows = slot_up_factor.reshape(doc_count * R, slot_up_factor.shape[2])
    raised_rows = frozen_output + LOWDIM_MULTIPLE * jnp.dot(
        broadcast_rows, up_factor_rows, preferred_element_type=jnp.float32
    )
    adapted = raised_rows.astype(jnp.bfloat16)
    residual = (raised_rows - targets.astype(jnp.float32)).astype(jnp.bfloat16)
    partial_up_gradient = LOWDIM_MULTIPLE * lax.dot_general(
        broadcast_rows, residual, (((0,), (0,)), ((), ())), preferred_element_type=jnp.float32
    )
    grad_up_local = lax.psum_scatter(
        partial_up_gradient.reshape(doc_count, R, up_factor_rows.shape[1]).astype(jnp.bfloat16),
        "tensor",
        scatter_dimension=2,
        tiled=True,
    ).astype(jnp.float32)
    document_list = lax.dot_general(
        residual, up_factor_rows, (((1,), (1,)), ((), ())), preferred_element_type=jnp.float32
    ).reshape(row_count, doc_count, R)
    token_portion = LOWDIM_MULTIPLE * jnp.sum(
        jnp.where(document_member[:, :, None], document_list, 0.0), axis=1
    )
    placed = lax.dynamic_update_slice_in_dim(
        jnp.zeros((token_count, R), jnp.float32), token_portion, row_start, 0
    )
    position_sensitivity = lax.psum(placed, ("tensor", "dp")).astype(jnp.bfloat16)
    lowering_matrix_sensitivity = fan_width_multiplier * jnp.einsum(
        "oed,oec->odc",
        position_sensitivity.reshape(doc_count, per_doc, R),
        bundled_entries,
        preferred_element_type=jnp.float32,
    )
    own_docs = group_start + jnp.arange(doc_count, dtype=jnp.int32)
    initial_grads = (
        jnp.zeros(
            (
                doc_count,
                lowering_matrix_sensitivity.shape[1] * lowering_matrix_sensitivity.shape[2],
            ),
            jnp.float32,
        ),
        jnp.zeros((doc_count, grad_up_local.shape[1] * grad_up_local.shape[2]), jnp.float32),
    )
    pieces = (
        lax.all_gather(
            lowering_matrix_sensitivity.astype(jnp.bfloat16), "group", axis=0, tiled=True
        ).astype(jnp.float32),
        lax.all_gather(grad_up_local.astype(jnp.bfloat16), "group", axis=0, tiled=True).astype(
            jnp.float32
        ),
    )
    piece_rows = pieces[0].shape[0]
    picker = (own_docs[:, None] == assign[None, :]).astype(jnp.float32)
    first = initial_grads[0] + jnp.dot(
        picker, pieces[0].reshape(piece_rows, -1), precision=lax.Precision.HIGHEST
    )
    second = initial_grads[1] + jnp.dot(
        picker, pieces[1].reshape(piece_rows, -1), precision=lax.Precision.HIGHEST
    )
    grad_down = first.reshape(lowering_matrix_sensitivity.shape)
    grad_up = second.reshape(grad_up_local.shape)
    return (adapted, grad_down, grad_up)


def solution(mesh):
    in_specs = (
        P("group", "dp"),
        P(None, "dp"),
        P("dp", "tensor"),
        P("tensor", "dp"),
        P(),
        P("group", "tensor"),
        P("tensor", "dp"),
        P(("group", "tensor"), "dp"),
    )
    out_specs = (
        P(("group", "tensor"), "dp"),
        P("group", None, "tensor"),
        P("group", None, ("dp", "tensor")),
    )
    return jax.shard_map(body, mesh=mesh, in_specs=in_specs, out_specs=out_specs, check_vma=False)
```

profile of v0, /device:TPU:0, one launch (start us, length us, event | category | flops | bytes accessed | tf_op | source)
XLA Modules:
  0.0 643.9 jit_solution(16494009230367694234)
XLA Ops:
  7.2 5.9 convolution_convert_fusion.2
  13.2 7.2 %all-gather = bf16[4,12,2048]{2,1,0:T(8,128)(2,1)S(1)} all-gather(bf16[1,12,2048]{2,1,0:T(8,128)(2,1)S(1)} %bitcast.83), channel_id=1, replica_groups=mesh['group'=4,'tensor'=4,'dp'=2] {'group'}, dimensions={0}, use_global_device_ids=true | all-gather | bytes 245760 | tf_op jit(solution)/shard_map/all_gather | solution.py:47
  20.6 4.8 convolution_convert_fusion.4
  25.4 8.9 %psum.35 = bf16[12,2048]{1,0:T(8,128)(2,1)S(1)} all-reduce(bf16[12,2048]{1,0:T(8,128)(2,1)S(1)} %convolution_convert_fusion.4), channel_id=1, replica_groups=mesh['group'=4,'tensor'=4,'dp'=2] {'dp'}, use_global_device_ids=true, to_apply=%region_1.0 | all-reduce | flops 24576 | bytes 98304 | tf_op jit(solution)/shard_map/psum | solution.py:20
  34.3 5.0 all-reduce.4.cloned.1.call-done
  42.8 18.5 %convolution_convert_fusion = bf16[768,4096]{1,0:T(8,128)(2,1)} fusion(bf16[768,2048]{1,0:T(8,128)(2,1)S(1)} %fusion.6, bf16[2048,4096]{1,0:T(8,128)(2,1)} %param.11), kind=kOutput, calls=%fused_computation | convolution fusion | flops 12888047616 | bytes 26214400 | tf_op jit(solution)/shard_map/dot_general | solution.py:31
  61.4 222.9 %all-reduce.6.cloned.1.call-done = bf16[12,64,4096]{2,1,0:T(8,128)(2,1)} async-done(((bf16[12,64,4096]{2,1,0:T(8,128)(2,1)}), bf16[12,64,4096]{2,1,0:T(8,128)(2,1)}) %all-reduce.6.cloned.1.call-update) | async-done | bytes 6291472 | tf_op jit(solution)/shard_map/psum | solution.py:32
  284.4 3.8 slice_select_fusion
  288.2 84.8 %all-reduce.8.cloned.1.call-done = bf16[12,32,4096]{2,1,0:T(8,128)(2,1)} async-done(((bf16[12,32,4096]{2,1,0:T(8,128)(2,1)}), bf16[12,32,4096]{2,1,0:T(8,128)(2,1)}) %all-reduce.8.cloned.1.call-update) | async-done | bytes 3145744 | tf_op jit(solution)/shard_map/psum | solution.py:14
  373.0 2.1 fusion.31
  376.2 15.0 %convolution_convert_fusion.1 = bf16[576,4096]{1,0:T(8,128)(2,1)} fusion(bf16[576,2048]{1,0:T(8,128)(2,1)S(1)} %copy-done, bf16[2048,4096]{1,0:T(8,128)(2,1)} %param.14), kind=kOutput, calls=%fused_computation.11 | convolution fusion | flops 9666035712 | bytes 23855104 | tf_op jit(solution)/shard_map/dot_general | solution.py:60
  391.3 4.4 reduce-scatter.10.cloned.1.call-done
  397.2 84.1 %reduce-scatter.6.cloned.1.call-done = bf16[144,4096]{1,0:T(8,128)(2,1)} async-done(((bf16[576,4096]{1,0:T(8,128)(2,1)}), bf16[144,4096]{1,0:T(8,128)(2,1)}) %reduce-scatter.6.cloned.1.call-update) | async-done | bytes 1179664 | tf_op jit(solution)/shard_map/reduce_scatter | solution.py:62
  481.4 4.1 fusion.47
  485.5 2.7 multiply_convert_fusion
  488.8 3.6 fusion.23
  492.9 40.6 %psum.39 = bf16[576,32]{0,1:T(8,128)(2,1)S(1)} all-reduce(f32[576,32]{0,1:T(8,128)S(1)} %dynamic_update_slice.3), channel_id=1, replica_groups=mesh['group'=4,'tensor'=4,'dp'=2] {'tensor','dp'}, use_global_device_ids=true, to_apply=%region_7.8 | all-reduce | flops 18432 | bytes 110592 | tf_op jit(solution)/shard_map/psum | solution.py:101
  535.7 15.1 %reduce-scatter.8.cloned.1.call-done = bf16[12,32,1024]{2,1,0:T(8,128)(2,1)} async-done(((bf16[12,32,4096]{2,1,0:T(8,128)(2,1)}), bf16[12,32,1024]{2,1,0:T(8,128)(2,1)}) %reduce-scatter.8.cloned.1.call-update) | async-done | bytes 786448 | tf_op jit(solution)/shard_map/reduce_scatter | solution.py:86
  550.8 48.7 %all-gather.4.cloned.1.call-done = bf16[48,32,2048]{2,1,0:T(8,128)(2,1)} async-done(((bf16[12,32,2048]{2,1,0:T(8,128)(2,1)}), bf16[48,32,2048]{2,1,0:T(8,128)(2,1)}) %all-gather.4.cloned.1.call-update) | async-done | bytes 6291472 | tf_op jit(solution)/shard_map/all_gather | solution.py:120
  599.6 9.6 %fusion = f32[12,32,2048]{2,0,1:T(8,128)S(1)} fusion(s32[48]{0:T(128)S(1)} %copy-done.8, s32[12]{0:T(128)S(1)} %iota_add_fusion, bf16[6,8,32,2048]{3,2,1,0:T(8,128)(2,1)} %bitcast.79), kind=kOutput, calls=%fused_computation.1 | convolution fusion | flops 75498048 | bytes 9437424 | tf_op jit(solution)/shard_map/dot_general | solution.py:129
  609.1 3.5 copy.23
  612.6 17.1 %all-gather.6.cloned.1.call-done = bf16[48,32,1024]{2,1,0:T(8,128)(2,1)} async-done(((bf16[12,32,1024]{2,1,0:T(8,128)(2,1)}), bf16[48,32,1024]{2,1,0:T(8,128)(2,1)}) %all-gather.6.cloned.1.call-update) | async-done | bytes 3145744 | tf_op jit(solution)/shard_map/all_gather | solution.py:123
  629.7 5.3 fusion.9
  635.0 2.1 copy.24
  (52 shorter events, 9.8 us)
Async XLA Ops:
  7.2 365.9 %copy-start = (bf16[576,2048]{1,0:T(8,128)(2,1)S(1)}, bf16[576,2048]{1,0:T(8,128)(2,1)}, u32[]{:S(2)}) copy-start(bf16[576,2048]{1,0:T(8,128)(2,1)} %param.13) | copy-start | bytes 7077892
  7.2 6.0 copy-start.4
  7.2 13.3 %copy-start.7 = (s32[48]{0:T(128)S(1)}, s32[48]{0:T(128)}, u32[]{:S(2)}) copy-start(s32[48]{0:T(128)} %param.12) | copy-start | bytes 580
  7.2 32.1 %all-reduce.4.cloned.1.call-start = ((), (), s32[]{:S(2)}) async-start(), calls=%async_computation.4 | async-start | bytes 524288 | tf_op jit(solution)/shard_map/psum | solution.py:24
  13.2 271.2 %all-reduce.6.cloned.1.call-start = ((), (), s32[]{:S(2)}) async-start(), calls=%async_computation.5 | async-start | bytes 12582912 | tf_op jit(solution)/shard_map/psum | solution.py:32
  61.4 311.7 %all-reduce.8.cloned.1.call-start = ((), (), s32[]{:S(2)}) async-start(), calls=%async_computation.6 | async-start | bytes 6291456 | tf_op jit(solution)/shard_map/psum | solution.py:14
  288.1 107.5 %reduce-scatter.10.cloned.1.call-start = ((), (), s32[]{:S(2)}) async-start(), calls=%async_computation.10 | async-start | bytes 184320
  376.0 105.4 %reduce-scatter.6.cloned.1.call-start = ((), (), s32[]{:S(2)}) async-start(), calls=%async_computation.3 | async-start | bytes 5898240 | tf_op jit(solution)/shard_map/reduce_scatter | solution.py:62
  391.2 159.6 %reduce-scatter.8.cloned.1.call-start = ((), (), s32[]{:S(2)}) async-start(), calls=%async_computation.8 | async-start | bytes 3932160 | tf_op jit(solution)/shard_map/reduce_scatter | solution.py:86
  391.3 5.3 copy-start.5
  397.2 88.2 %copy-start.2 = (bf16[144,4096]{1,0:T(8,128)(2,1)S(1)}, bf16[144,4096]{1,0:T(8,128)(2,1)}, u32[]{:S(2)}) copy-start(bf16[144,4096]{1,0:T(8,128)(2,1)} %param.15) | copy-start | bytes 3538948
  481.4 4.1 copy-start.3
  485.5 2.7 copy-start.1
  488.2 0.7 copy-start.6
  488.2 111.4 %all-gather.4.cloned.1.call-start = ((), (), s32[]{:S(2)}) async-start(), calls=%async_computation.7 | async-start | bytes 7864320 | tf_op jit(solution)/shard_map/all_gather | solution.py:120
  533.7 65.9 %copy-start.8 = (s32[48]{0:T(128)S(1)}, s32[48]{0:T(128)}, u32[]{:S(2)}) copy-start(s32[48]{0:T(128)} %param.12) | copy-start | bytes 580
  535.4 94.2 %all-gather.6.cloned.1.call-start = ((), (), s32[]{:S(2)}) async-start(), calls=%async_computation.9 | async-start | bytes 3932160 | tf_op jit(solution)/shard_map/all_gather | solution.py:123
Sparse Core Ops, SparseCore 0:
  13.3 26.0 all-reduce.3
  61.5 222.8 all-reduce.5
  288.3 84.7 all-reduce.7
  376.1 19.5 reduce-scatter.9
  397.8 83.4 reduce-scatter.5
  488.3 62.4 reduce-scatter.7
  552.9 46.5 all-gather.3
  601.1 28.4 all-gather.5
where the time goes:
time: 644 us
  waiting for transfers between devices  482 us (75%)
  matrix products  73.3 us (11%)
  blocking collectives  56.7 us (9%)
  between operations  14.4 us (2%)
  local copies, waits for them, and re-layouts  8.55 us (1%)
  other arithmetic  7.99 us (1%)
    psum x1, waiting for transfers between devices, hypernet(): summed = lax.psum(partial_value.astype(jnp.bfloat16), 'tensor')  223 us
    psum x1, waiting for transfers between devices, spread(): return lax.psum(block, axis)  84.8 us
    reduce_scatter x1, waiting for transfers between devices, body(): lax.psum_scatter(base_part.astype(jnp.bfloat16), 'tensor', scatter_dimens...  84.1 us
    all_gather x1, waiting for transfers between devices, body(): lax.all_gather(lowering_matrix_sensitivity.astype(jnp.bfloat16), 'group',...  48.7 us
    psum x1, blocking collectives, body(): lax.psum(placed, ('tensor', 'dp')).astype(jnp.bfloat16)  40.6 us
    dot_general x1, matrix products, hypernet(): jnp.dot(hidden, hyper_out, preferred_element_type=jnp.float32)  18.5 us
    all_gather x1, waiting for transfers between devices, body(): lax.all_gather(grad_up_local.astype(jnp.bfloat16), 'group', axis=0, tiled...  17.1 us
    reduce_scatter x1, waiting for transfers between devices, body(): lax.psum_scatter(partial_up_gradient.reshape(doc_count, R, up_factor_rows...  15.1 us
  transfers between devices with their start and end apart: 8, of which 8 were waited for; matrix products, arithmetic and copies ran while one was open for 6% of the time, Pallas kernels for 0%

commit v1 on v0

--- a/solution.py
+++ b/solution.py
@@ -98,7 +98,7 @@
     placed = lax.dynamic_update_slice_in_dim(
         jnp.zeros((token_count, R), jnp.float32), token_portion, row_start, 0
     )
-    position_sensitivity = lax.psum(placed, ("tensor", "dp")).astype(jnp.bfloat16)
+    position_sensitivity = lax.psum(lax.psum(placed, axis_name="dp"), "tensor").astype(jnp.bfloat16)
     lowering_matrix_sensitivity = fan_width_multiplier * jnp.einsum(
         "oed,oec->odc",
         position_sensitivity.reshape(doc_count, per_doc, R),

time: 644 us -> 671 us (1.042)
  waiting for transfers between devices: 482 us -> 524 us
  blocking collectives: 56.7 us -> 38.4 us
    reduce_scatter x1, waiting for transfers between devices: 15.1 us -> 39.6 us  [body(): lax.psum_scatter(partial_up_gradient.reshape(doc_count, R, up_factor_rows...]
    psum x1, blocking collectives: 40.6 us -> 22.3 us  [body(): lax.psum(lax.psum(placed, axis_name='dp'), 'tensor').astype(jnp.bfloat16)]
    psum x0 -> x1, waiting for transfers between devices: none -> 17.3 us  [body(): lax.psum(placed, axis_name='dp')]
  transfers between devices with their start and end apart: 8 -> 9, of which waited for: 8 -> 9; matrix products, arithmetic and copies ran while one was open for 6% -> 6% of each run, Pallas kernels for 0% -> 0%
where the time goes in v1:
time: 671 us
  waiting for transfers between devices  524 us (78%)
  matrix products  75.2 us (11%)
  blocking collectives  38.4 us (6%)
  between operations  14.1 us (2%)
  local copies, waits for them, and re-layouts  9.54 us (1%)
  other arithmetic  8.6 us (1%)
    psum x1, waiting for transfers between devices, hypernet(): summed = lax.psum(partial_value.astype(jnp.bfloat16), 'tensor')  223 us
    psum x1, waiting for transfers between devices, spread(): return lax.psum(block, axis)  84.8 us
    reduce_scatter x1, waiting for transfers between devices, body(): lax.psum_scatter(base_part.astype(jnp.bfloat16), 'tensor', scatter_dimens...  84.1 us
    all_gather x1, waiting for transfers between devices, body(): lax.all_gather(lowering_matrix_sensitivity.astype(jnp.bfloat16), 'group',...  48.7 us
    reduce_scatter x1, waiting for transfers between devices, body(): lax.psum_scatter(partial_up_gradient.reshape(doc_count, R, up_factor_rows...  39.6 us
    psum x1, blocking collectives, body(): lax.psum(lax.psum(placed, axis_name='dp'), 'tensor').astype(jnp.bfloat16)  22.3 us
    dot_general x1, matrix products, hypernet(): jnp.dot(hidden, hyper_out, preferred_element_type=jnp.float32)  18.5 us
    psum x1, waiting for transfers between devices, body(): lax.psum(placed, axis_name='dp')  17.3 us
  transfers between devices with their start and end apart: 9, of which 9 were waited for; matrix products, arithmetic and copies ran while one was open for 6% of the time, Pallas kernels for 0%

profile of v1, /device:TPU:0, one launch (start us, length us, event | category | flops | bytes accessed | tf_op | source)
XLA Modules:
  0.0 670.7 jit_solution(14541440390857032090)
XLA Ops:
  7.2 5.9 convolution_convert_fusion.2
  13.2 7.2 %all-gather = bf16[4,12,2048]{2,1,0:T(8,128)(2,1)S(1)} all-gather(bf16[1,12,2048]{2,1,0:T(8,128)(2,1)S(1)} %bitcast.83), channel_id=1, replica_groups=mesh['group'=4,'tensor'=4,'dp'=2] {'group'}, dimensions={0}, use_global_device_ids=true | all-gather | bytes 245760 | tf_op jit(solution)/shard_map/all_gather | solution.py:47
  20.6 4.8 convolution_convert_fusion.4
  25.4 8.9 %psum.42 = bf16[12,2048]{1,0:T(8,128)(2,1)S(1)} all-reduce(bf16[12,2048]{1,0:T(8,128)(2,1)S(1)} %convolution_convert_fusion.4), channel_id=1, replica_groups=mesh['group'=4,'tensor'=4,'dp'=2] {'dp'}, use_global_device_ids=true, to_apply=%region_1.0 | all-reduce | flops 24576 | bytes 98304 | tf_op jit(solution)/shard_map/psum | solution.py:20
  34.3 5.0 all-reduce.5.cloned.1.call-done
  42.8 18.5 %convolution_convert_fusion = bf16[768,4096]{1,0:T(8,128)(2,1)} fusion(bf16[768,2048]{1,0:T(8,128)(2,1)S(1)} %fusion.6, bf16[2048,4096]{1,0:T(8,128)(2,1)} %param.11), kind=kOutput, calls=%fused_computation | convolution fusion | flops 12888047616 | bytes 26214400 | tf_op jit(solution)/shard_map/dot_general | solution.py:31
  61.4 222.9 %all-reduce.7.cloned.1.call-done = bf16[12,64,4096]{2,1,0:T(8,128)(2,1)} async-done(((bf16[12,64,4096]{2,1,0:T(8,128)(2,1)}), bf16[12,64,4096]{2,1,0:T(8,128)(2,1)}) %all-reduce.7.cloned.1.call-update) | async-done | bytes 6291472 | tf_op jit(solution)/shard_map/psum | solution.py:32
  284.3 3.8 slice_select_fusion
  288.2 84.8 %all-reduce.9.cloned.1.call-done = bf16[12,32,4096]{2,1,0:T(8,128)(2,1)} async-done(((bf16[12,32,4096]{2,1,0:T(8,128)(2,1)}), bf16[12,32,4096]{2,1,0:T(8,128)(2,1)}) %all-reduce.9.cloned.1.call-update) | async-done | bytes 3145744 | tf_op jit(solution)/shard_map/psum | solution.py:14
  373.0 2.1 fusion.31
  376.2 15.0 %convolution_convert_fusion.1 = bf16[576,4096]{1,0:T(8,128)(2,1)} fusion(bf16[576,2048]{1,0:T(8,128)(2,1)S(1)} %copy-done, bf16[2048,4096]{1,0:T(8,128)(2,1)} %param.14), kind=kOutput, calls=%fused_computation.11 | convolution fusion | flops 9666035712 | bytes 23855104 | tf_op jit(solution)/shard_map/dot_general | solution.py:60
  391.3 4.4 reduce-scatter.10.cloned.1.call-done
  397.2 84.1 %reduce-scatter.6.cloned.1.call-done = bf16[144,4096]{1,0:T(8,128)(2,1)} async-done(((bf16[576,4096]{1,0:T(8,128)(2,1)}), bf16[144,4096]{1,0:T(8,128)(2,1)}) %reduce-scatter.6.cloned.1.call-update) | async-done | bytes 1179664 | tf_op jit(solution)/shard_map/reduce_scatter | solution.py:62
  481.3 4.1 fusion.47
  485.4 3.8 fusion.23
  492.0 4.4 multiply_convert_fusion
  496.5 17.3 %all-reduce.11.cloned.1.call-done = f32[576,32]{0,1:T(8,128)} async-done(((f32[576,32]{0,1:T(8,128)}), f32[576,32]{0,1:T(8,128)}) %all-reduce.11.cloned.1.call-update) | async-done | bytes 73744 | tf_op jit(solution)/shard_map/psum | solution.py:101
  513.8 22.3 %psum.47 = bf16[576,32]{0,1:T(8,128)(2,1)S(1)} all-reduce(f32[576,32]{0,1:T(8,128)} %all-reduce.11.cloned.1.call-done), channel_id=1, replica_groups=mesh['group'=4,'tensor'=4,'dp'=2] {'tensor'}, use_global_device_ids=true, to_apply=%region_8.9 | all-reduce | flops 18432 | bytes 110592 | tf_op jit(solution)/shard_map/psum | solution.py:101
  538.3 39.6 %reduce-scatter.8.cloned.1.call-done = bf16[12,32,1024]{2,1,0:T(8,128)(2,1)} async-done(((bf16[12,32,4096]{2,1,0:T(8,128)(2,1)}), bf16[12,32,1024]{2,1,0:T(8,128)(2,1)}) %reduce-scatter.8.cloned.1.call-update) | async-done | bytes 786448 | tf_op jit(solution)/shard_map/reduce_scatter | solution.py:86
  577.9 48.7 %all-gather.4.cloned.1.call-done = bf16[48,32,2048]{2,1,0:T(8,128)(2,1)} async-done(((bf16[12,32,2048]{2,1,0:T(8,128)(2,1)}), bf16[48,32,2048]{2,1,0:T(8,128)(2,1)}) %all-gather.4.cloned.1.call-update) | async-done | bytes 6291472 | tf_op jit(solution)/shard_map/all_gather | solution.py:120
  626.7 9.6 %fusion = f32[12,32,2048]{2,0,1:T(8,128)S(1)} fusion(s32[48]{0:T(128)S(1)} %copy-done.7, s32[12]{0:T(128)S(1)} %iota_add_fusion, bf16[6,8,32,2048]{3,2,1,0:T(8,128)(2,1)} %bitcast.79), kind=kOutput, calls=%fused_computation.1 | convolution fusion | flops 75498048 | bytes 9437424 | tf_op jit(solution)/shard_map/dot_general | solution.py:129
  636.3 3.5 copy.23
  639.7 17.1 %all-gather.6.cloned.1.call-done = bf16[48,32,1024]{2,1,0:T(8,128)(2,1)} async-done(((bf16[12,32,1024]{2,1,0:T(8,128)(2,1)}), bf16[48,32,1024]{2,1,0:T(8,128)(2,1)}) %all-gather.6.cloned.1.call-update) | async-done | bytes 3145744 | tf_op jit(solution)/shard_map/all_gather | solution.py:123
  656.8 5.3 fusion.9
  (53 shorter events, 13.5 us)
Async XLA Ops:
  7.2 365.8 %copy-start = (bf16[576,2048]{1,0:T(8,128)(2,1)S(1)}, bf16[576,2048]{1,0:T(8,128)(2,1)}, u32[]{:S(2)}) copy-start(bf16[576,2048]{1,0:T(8,128)(2,1)} %param.13) | copy-start | bytes 7077892
  7.2 6.0 copy-start.3
  7.2 13.3 %copy-start.6 = (s32[48]{0:T(128)S(1)}, s32[48]{0:T(128)}, u32[]{:S(2)}) copy-start(s32[48]{0:T(128)} %param.12) | copy-start | bytes 580
  7.2 32.1 %all-reduce.5.cloned.1.call-start = ((), (), s32[]{:S(2)}) async-start(), calls=%async_computation.4 | async-start | bytes 524288 | tf_op jit(solution)/shard_map/psum | solution.py:24
  13.2 271.2 %all-reduce.7.cloned.1.call-start = ((), (), s32[]{:S(2)}) async-start(), calls=%async_computation.5 | async-start | bytes 12582912 | tf_op jit(solution)/shard_map/psum | solution.py:32
  61.3 311.7 %all-reduce.9.cloned.1.call-start = ((), (), s32[]{:S(2)}) async-start(), calls=%async_computation.6 | async-start | bytes 6291456 | tf_op jit(solution)/shard_map/psum | solution.py:14
  288.1 107.5 %reduce-scatter.10.cloned.1.call-start = ((), (), s32[]{:S(2)}) async-start(), calls=%async_computation.11 | async-start | bytes 184320
  376.0 105.3 %reduce-scatter.6.cloned.1.call-start = ((), (), s32[]{:S(2)}) async-start(), calls=%async_computation.3 | async-start | bytes 5898240 | tf_op jit(solution)/shard_map/reduce_scatter | solution.py:62
  391.2 122.6 %all-reduce.11.cloned.1.call-start = ((), (), s32[]{:S(2)}) async-start(), calls=%async_computation.7 | async-start | bytes 163840 | tf_op jit(solution)/shard_map/psum | solution.py:101
  391.3 5.3 copy-start.4
  397.2 88.2 %copy-start.2 = (bf16[144,4096]{1,0:T(8,128)(2,1)S(1)}, bf16[144,4096]{1,0:T(8,128)(2,1)}, u32[]{:S(2)}) copy-start(bf16[144,4096]{1,0:T(8,128)(2,1)} %param.15) | copy-start | bytes 3538948
  481.3 4.1 copy-start.5
  485.4 3.8 copy-start.1
  491.9 86.0 %reduce-scatter.8.cloned.1.call-start = ((), (), s32[]{:S(2)}) async-start(), calls=%async_computation.9 | async-start | bytes 3932160 | tf_op jit(solution)/shard_map/reduce_scatter | solution.py:86
  496.4 130.3 %all-gather.4.cloned.1.call-start = ((), (), s32[]{:S(2)}) async-start(), calls=%async_computation.8 | async-start | bytes 7864320 | tf_op jit(solution)/shard_map/all_gather | solution.py:120
  536.2 90.5 %copy-start.7 = (s32[48]{0:T(128)S(1)}, s32[48]{0:T(128)}, u32[]{:S(2)}) copy-start(s32[48]{0:T(128)} %param.12) | copy-start | bytes 580
  538.0 118.8 %all-gather.6.cloned.1.call-start = ((), (), s32[]{:S(2)}) async-start(), calls=%async_computation.10 | async-start | bytes 3932160 | tf_op jit(solution)/shard_map/all_gather | solution.py:123
Sparse Core Ops, SparseCore 0:
  13.3 26.0 all-reduce.4
  61.5 222.8 all-reduce.6
  288.3 84.7 all-reduce.8
  376.1 19.5 reduce-scatter.9
  397.8 83.4 reduce-scatter.5
  492.0 21.7 all-reduce.10
  516.7 61.1 reduce-scatter.7
  580.0 46.6 all-gather.3
  628.3 28.4 all-gather.5
